TPU v7x, 1024 devices: a whole 4x4x32 slice. The times are simulated.
1024 devices in a mesh: seq: 64 (over y, z_lo), fsdp: 8 (over z_hi, x), grp: 2 (over core).
Axes of the slice: x: 4, y: 4, z: 32 (z_hi: 2, z_lo: 16; z = z_hi * 16 + z_lo), core: 2. Of those that a mesh axis runs over, the one named last changes fastest.
Arguments:
- queries: bfloat16 [1, 65536, 2048], P(None, ('seq', 'fsdp'), 'grp'), may hold values from -208 to 208
- encodings: bfloat16 [1, 1024, 2, 128, 896], P(None, ('seq', 'fsdp'), None, 'grp'), may hold values from -6 to 6
- neighbour_lengths: int32 [1, 1024, 2], P(None, ('seq', 'fsdp')), may hold values from 32 to 128
- key_weight: bfloat16 [896, 2048], P(None, 'grp'), may hold values from -0.1875 to 0.1875
- value_weight: bfloat16 [896, 2048], P(None, 'grp'), may hold values from -0.1875 to 0.1875
Outputs:
- attended: bfloat16 [1, 65536, 2048], P(None, ('seq', 'fsdp'), 'grp')
All inputs are finite; a program needn't handle non-finite values.
Results may differ from a plain program's by a relative error of at most 0.011.
Values may be sent and summed in bfloat16 or wider, within the bound.
A program may use at most 32 MiB of HBM per device.

v0:
```python
import jax
import jax.numpy as jnp
from jax import lax
from jax.sharding import PartitionSpec as P

HEAD_DIM = 128


mask_fill = -1e30


def shifted(array, axis, by):
    size = lax.axis_size(axis)
    pairs = [(i, i + by) for i in range(size) if 0 <= i + by < size]
    return lax.ppermute(array, axis, pairs)


def attend_blocks(query_blocks, key_value, lengths):
    seq_count, block_count, row_count, col_count = query_blocks.shape
    head_count = col_count // HEAD_DIM
    key_count = key_value.shape[3] * key_value.shape[4]
    softmax_scale = HEAD_DIM ** (-0.5)
    query_heads = query_blocks.reshape(seq_count, block_count, row_count, head_count, HEAD_DIM)
    key_rows = key_value[0].reshape(seq_count, block_count, key_count, head_count, HEAD_DIM)
    value_rows = key_value[1].reshape(seq_count, block_count, key_count, head_count, HEAD_DIM)
    scores = (
        jnp.einsum("bnqhd,bnkhd->bnhqk", query_heads, key_rows, preferred_element_type=jnp.float32)
        * softmax_scale
    )
    position = lax.broadcasted_iota(jnp.float32, key_value.shape[1:5], 3)
    key_live = (position < lengths[..., None]).reshape(seq_count, block_count, 1, 1, key_count)
    scores = jnp.where(key_live, scores, mask_fill)
    row_max = jnp.max(scores, axis=-1, keepdims=True)
    weights = jnp.exp(scores - row_max)
    attention = (weights / jnp.sum(weights, axis=-1, keepdims=True)).astype(jnp.bfloat16)
    attended = jnp.einsum(
        "bnhqk,bnkhd->bnqhd", attention, value_rows, preferred_element_type=jnp.float32
    )
    return attended.astype(jnp.bfloat16).reshape(seq_count, block_count * row_count, col_count)


def attend_padded(queries, all_pairs, all_lengths, group_count, group_len):
    seq_count, tok_count, col_count = queries.shape
    lead_zeros = jnp.zeros((seq_count, 1, col_count), jnp.bfloat16)
    trail_zeros = jnp.zeros((seq_count, group_len - 1, col_count), jnp.bfloat16)
    padded = jnp.concatenate([lead_zeros, queries, trail_zeros], axis=1)
    blocks = padded.reshape(seq_count, group_count + 1, group_len, col_count)
    attended = attend_blocks(blocks, all_pairs, all_lengths)
    return attended[:, 1 : 1 + tok_count]


def shards(queries, encodings, neighbour_lengths, key_weight, value_weight):
    seq_count, tok_count, col_count = queries.shape
    group_count = encodings.shape[1]
    group_len = tok_count // group_count
    enc_width = encodings.shape[4]
    lengths = neighbour_lengths.astype(jnp.float32)
    shard_rows = lax.all_gather(encodings, "grp", axis=3, tiled=True)
    flat_rows = shard_rows.reshape(-1, enc_width)
    key_part = jnp.dot(flat_rows, key_weight, preferred_element_type=jnp.float32).astype(
        jnp.bfloat16
    )
    value_part = jnp.dot(flat_rows, value_weight, preferred_element_type=jnp.float32).astype(
        jnp.bfloat16
    )
    key_value = jnp.stack([key_part, value_part]).reshape(
        (2,) + shard_rows.shape[:4] + (col_count,)
    )
    last_pair = key_value[:, :, group_count - 1]
    last_lengths = neighbour_lengths[:, group_count - 1].astype(jnp.bfloat16)
    prev_pair, prev_lengths = shifted((last_pair, last_lengths), ("seq", "fsdp"), 1)
    all_pairs = jnp.concatenate([prev_pair[:, :, None], key_value], axis=2)
    all_lengths = jnp.concatenate([prev_lengths.astype(jnp.float32)[:, None], lengths], axis=1)
    return attend_padded(queries, all_pairs, all_lengths, group_count, group_len)


def solution(mesh):
    placed = (
        P(None, ("seq", "fsdp"), "grp"),
        P(None, ("seq", "fsdp"), None, "grp", None),
        P(None, ("seq", "fsdp"), None),
        P(None, "grp"),
        P(None, "grp"),
    )
    return jax.shard_map(
        shards,
        mesh=mesh,
        in_specs=placed,
        out_specs=P(None, ("seq", "fsdp"), "grp"),
        check_vma=False,
    )
```

profile of v0, /device:TPU:40, one launch (start us, length us, event | category | flops | bytes accessed | tf_op | source)
XLA Modules:
  0.0 384.9 jit_solution(9286696181366929941)
XLA Ops:
  0.0 0.0 copy-start
  0.0 2.8 all_gather.3
  2.8 0.0 copy-done
  2.8 0.0 copy-start.3
  2.8 1.3 convolution_convert_fusion.1
  4.1 0.2 copy-done.3
  4.3 1.2 convolution_convert_fusion
  5.6 0.0 copy-start.2
  5.6 0.0 copy-start.1
  5.6 0.1 fusion.15
  5.7 3.4 collective-permute-start
  9.1 0.0 copy-done.2
  9.1 3.4 collective-permute-start.1
  12.5 0.1 pad.7.clone
  12.6 0.0 copy-done.1
  12.6 0.2 maximum_bitcast_fusion
  12.8 0.1 copy.18
  12.9 360.8 %collective-permute-done.1 = bf16[1,2]{1,0:T(2,128)(2,1)S(1)} collective-permute-done((bf16[1,2]{1,0:T(2,128)(2,1)S(1)}, bf16[1,2]{1,0:T(2,128)(2,1)S(1)}, u32[]{:S(2)}, u32[]{:S(2)}) %collective-permute-start.1) | collective-permute-done | bytes 36 | tf_op jit(solution)/shard_map/ppermute | solution.py:15
  373.8 0.1 broadcast_bitcast_fusion
  373.9 0.0 collective-permute-done
  373.9 0.3 maximum_maximum_fusion
  374.2 0.3 fusion.19
  374.5 0.4 copy.19
  375.0 0.7 multiply_select_fusion
  375.7 0.5 fusion.21
  376.2 1.6 copy.20
  377.8 4.9 %fusion.12 = bf16[1,3,64,8,128]{4,2,3,1,0:T(8,128)(2,1)} fusion(bf16[3,256,8,128]{3,2,1,0:T(8,128)(2,1)} %bitcast.56, f32[3,8,64]{2,1,0:T(8,128)S(1)} %fusion.21, f32[3,8,64,256]{3,2,1,0:T(8,128)S(1)} %multiply_select_fusion), kind=kOutput, calls=%fused_computation.13 | convolution fusion | flops 102041344 | bytes 3545088 | tf_op jit(solution)/shard_map/bnhqk,bnkhd->bnqhd/dot_general | solution.py:36
  382.7 1.3 copy.15
  383.9 0.2 reshape.85
  384.1 0.8 slice.23
  (8 shorter events, 0.1 us)
Async XLA Ops:
  0.0 2.8 copy-start
  2.8 1.5 copy-start.3
  5.6 3.5 copy-start.2
  5.6 7.1 %copy-start.1 = (bf16[1,128,1024]{2,1,0:T(8,128)(2,1)S(1)}, bf16[1,128,1024]{2,1,0:T(8,128)(2,1)}, u32[]{:S(2)}) copy-start(bf16[1,128,1024]{2,1,0:T(8,128)(2,1)} %param.5) | copy-start | bytes 786436
  5.7 368.2 %collective-permute-start = (bf16[2,1,2,128,1024]{4,3,2,0,1:T(8,128)(2,1)S(1)}, bf16[2,1,2,128,1024]{4,3,2,0,1:T(8,128)(2,1)S(1)}, u32[]{:S(2)}, u32[]{:S(2)}) collective-permute-start(bf16[2,1,2,128,1024]{4,3,2,0,1:T(8,128)(2,1)S(1)} %fusion.15), channel_id=1, source_target_pairs={{0,2},{2,4},{4,6},{6,8},{8,10},{10,12},{12,14},{14,16},{16,18},{18... | collective-permute-start | bytes 3145736 | tf_op jit(solution)/shard_map/ppermute | solution.py:15
  9.1 364.6 %collective-permute-start.1 = (bf16[1,2]{1,0:T(2,128)(2,1)S(1)}, bf16[1,2]{1,0:T(2,128)(2,1)S(1)}, u32[]{:S(2)}, u32[]{:S(2)}) collective-permute-start(bf16[1,2]{1,0:T(2,128)(2,1)S(1)} %slice_bitcast_fusion), channel_id=1, source_target_pairs={{0,2},{2,4},{4,6},{6,8},{8,10},{10,12},{12,14},{14,16},{16,18},{18... | collective-permute-start | bytes 20 | tf_op jit(solution)/shard_map/ppermute | solution.py:15
where the time goes:
time: 385 us
  waiting for transfers between devices  361 us (94%)
  matrix products  8.11 us (2%)
  starting transfers between devices  6.8 us (2%)
  local copies, waits for them, and re-layouts  5.01 us (1%)
    ppermute x2, waiting for transfers between devices, shifted(): return lax.ppermute(array, axis, pairs)  361 us
  transfers between devices with their start and end apart: 2, of which 1 were waited for; matrix products, arithmetic and copies ran while one was open for 0% of the time, Pallas kernels for 0%

commit v1 on v0

--- a/solution.py
+++ b/solution.py
@@ -54,23 +54,21 @@
     group_count = encodings.shape[1]
     group_len = tok_count // group_count
     enc_width = encodings.shape[4]
-    lengths = neighbour_lengths.astype(jnp.float32)
-    shard_rows = lax.all_gather(encodings, "grp", axis=3, tiled=True)
-    flat_rows = shard_rows.reshape(-1, enc_width)
-    key_part = jnp.dot(flat_rows, key_weight, preferred_element_type=jnp.float32).astype(
-        jnp.bfloat16
-    )
-    value_part = jnp.dot(flat_rows, value_weight, preferred_element_type=jnp.float32).astype(
-        jnp.bfloat16
-    )
-    key_value = jnp.stack([key_part, value_part]).reshape(
-        (2,) + shard_rows.shape[:4] + (col_count,)
-    )
-    last_pair = key_value[:, :, group_count - 1]
-    last_lengths = neighbour_lengths[:, group_count - 1].astype(jnp.bfloat16)
-    prev_pair, prev_lengths = shifted((last_pair, last_lengths), ("seq", "fsdp"), 1)
-    all_pairs = jnp.concatenate([prev_pair[:, :, None], key_value], axis=2)
-    all_lengths = jnp.concatenate([prev_lengths.astype(jnp.float32)[:, None], lengths], axis=1)
+    last_rows = encodings[:, group_count - 1 :]
+    last_lengths = neighbour_lengths[:, group_count - 1 :]
+    prev_rows, prev_lengths = shifted((last_rows, last_lengths), ("seq", "fsdp"), 1)
+
+    def project(rows):
+        rows = lax.all_gather(rows, "grp", axis=3, tiled=True)
+        flat_rows = rows.reshape(-1, enc_width)
+        pair = [
+            jnp.dot(flat_rows, weight, preferred_element_type=jnp.float32).astype(jnp.bfloat16)
+            for weight in (key_weight, value_weight)
+        ]
+        return jnp.stack(pair).reshape((2,) + rows.shape[:4] + (col_count,))
+
+    all_pairs = jnp.concatenate([project(prev_rows), project(encodings)], axis=2)
+    all_lengths = jnp.concatenate([prev_lengths, neighbour_lengths], axis=1).astype(jnp.float32)
     return attend_padded(queries, all_pairs, all_lengths, group_count, group_len)
 
 

time: 385 us -> 121 us (0.31)
  the two profiles are of different devices: /device:TPU:40 before, /device:TPU:33 now
where the time goes in v1:
time: 121 us
  waiting for transfers between devices  90.5 us (75%)
  matrix products  9.6 us (8%)
  local copies, waits for them, and re-layouts  6.77 us (6%)
  blocking collectives  6.29 us (5%)
  starting transfers between devices  6.23 us (5%)
    ppermute x2, waiting for transfers between devices, shifted(): return lax.ppermute(array, axis, pairs)  90.5 us
    all_gather x2, blocking collectives, project(): rows = lax.all_gather(rows, 'grp', axis=3, tiled=True)  6.29 us
    ppermute x2, starting transfers between devices, shifted(): return lax.ppermute(array, axis, pairs)  6.23 us
    dot_general x1, matrix products, attend_blocks(): jnp.einsum('bnhqk,bnkhd->bnqhd', attention, value_rows, preferred_element...  4.9 us
    dot_general x4, matrix products, project(): jnp.dot(flat_rows, weight, preferred_element_type=jnp.float32)  4.02 us
  transfers between devices with their start and end apart: 2, of which 1 were waited for; matrix products, arithmetic and copies ran while one was open for 3% of the time, Pallas kernels for 0%

profile of v1, /device:TPU:33, one launch (start us, length us, event | category | flops | bytes accessed | tf_op | source)
XLA Modules:
  0.0 120.6 jit_solution(11664290469056371583)
XLA Ops:
  0.0 0.0 copy-start
  0.0 1.1 slice.15
  1.1 3.1 %collective-permute-start = (bf16[1,1,2,64,896]{4,3,2,1,0:T(8,128)(2,1)S(1)}, bf16[1,1,2,64,896]{4,3,2,1,0:T(8,128)(2,1)S(1)}, u32[]{:S(2)}, u32[]{:S(2)}) collective-permute-start(bf16[1,1,2,64,896]{4,3,2,1,0:T(8,128)(2,1)S(1)} %slice.15), channel_id=1, source_target_pairs={{0,2},{2,4},{4,6},{6,8},{8,10},{10,12},{12,14},{14,16},{16,18},{18... | collective-permute-start | bytes 688136 | tf_op jit(solution)/shard_map/ppermute | solution.py:15
  4.2 0.7 slice.17
  4.9 3.1 %collective-permute-start.1 = (s32[1,1,2]{2,1,0:T(1,128)S(1)}, s32[1,1,2]{2,1,0:T(1,128)S(1)}, u32[]{:S(2)}, u32[]{:S(2)}) collective-permute-start(s32[1,1,2]{2,1,0:T(1,128)S(1)} %slice.17), channel_id=1, source_target_pairs={{0,2},{2,4},{4,6},{6,8},{8,10},{10,12},{12,14},{14,16},{16,18},{18... | collective-permute-start | bytes 32 | tf_op jit(solution)/shard_map/ppermute | solution.py:15
  8.0 3.5 %all_gather.7 = bf16[1,2,2,128,896]{4,3,2,1,0:T(8,128)(2,1)S(1)} all-gather(bf16[1,2,2,64,896]{4,3,2,1,0:T(8,128)(2,1)} %param.6), channel_id=1, replica_groups=mesh['seq'=64,'fsdp'=8,'grp'=2] {'grp'}, dimensions={3}, use_global_device_ids=true | all-gather | bytes 1376256 | tf_op jit(solution)/shard_map/all_gather | solution.py:62
  11.6 0.0 copy-done
  11.6 0.0 copy-start.3
  11.6 1.3 %convolution_convert_fusion.1 = bf16[512,1024]{1,0:T(8,128)(2,1)S(1)} fusion(bf16[512,896]{1,0:T(8,128)(2,1)S(1)} %bitcast.53, bf16[896,1024]{1,0:T(8,128)(2,1)S(1)} %copy-done), kind=kOutput, calls=%fused_computation.11 | convolution fusion | flops 940048384 | bytes 3801088 | tf_op jit(solution)/shard_map/dot_general | solution.py:65
  12.9 0.2 copy-done.3
  13.1 1.3 %convolution_convert_fusion = bf16[512,1024]{1,0:T(8,128)(2,1)S(1)} fusion(bf16[512,896]{1,0:T(8,128)(2,1)S(1)} %bitcast.54, bf16[896,1024]{1,0:T(8,128)(2,1)S(1)} %copy-done.3), kind=kOutput, calls=%fused_computation.10 | convolution fusion | flops 940048384 | bytes 3801088 | tf_op jit(solution)/shard_map/dot_general | solution.py:65
  14.4 0.1 pad.6.clone
  14.4 0.0 copy-done.1
  14.4 0.2 maximum_bitcast_fusion
  14.7 0.1 copy.11
  14.7 90.5 %collective-permute-done.1 = s32[1,1,2]{2,1,0:T(1,128)S(1)} collective-permute-done((s32[1,1,2]{2,1,0:T(1,128)S(1)}, s32[1,1,2]{2,1,0:T(1,128)S(1)}, u32[]{:S(2)}, u32[]{:S(2)}) %collective-permute-start.1) | collective-permute-done | bytes 40 | tf_op jit(solution)/shard_map/ppermute | solution.py:15
  105.2 0.0 copy-done.2
  105.2 0.1 broadcast_bitcast_fusion
  105.3 0.0 collective-permute-done
  105.3 2.8 %all_gather.6 = bf16[1,1,2,128,896]{4,3,2,1,0:T(8,128)(2,1)S(1)} all-gather(bf16[1,1,2,64,896]{4,3,2,1,0:T(8,128)(2,1)S(1)} %collective-permute-done), channel_id=1, replica_groups=mesh['seq'=64,'fsdp'=8,'grp'=2] {'grp'}, dimensions={3}, use_global_device_ids=true | all-gather | bytes 688128 | tf_op jit(solution)/shard_map/all_gather | solution.py:62
  108.1 0.7 convolution_convert_fusion.3
  108.8 0.7 convolution_convert_fusion.2
  109.6 0.3 maximum_maximum_fusion
  109.9 0.3 fusion.18
  110.2 0.4 copy.12
  110.7 0.7 multiply_select_fusion
  111.3 0.5 fusion.19
  111.8 1.6 %copy.13 = bf16[96,8,8,128]{3,2,1,0:T(8,128)(2,1)} copy(bf16[96,8,8,128]{3,1,2,0:T(8,128)(2,1)S(1)} %bitcast.46) | data formatting | bytes 3145728
  113.4 4.9 %fusion.12 = bf16[1,3,64,8,128]{4,2,3,1,0:T(8,128)(2,1)} fusion(bf16[3,256,8,128]{3,2,1,0:T(8,128)(2,1)} %bitcast.49, f32[3,8,64]{2,1,0:T(8,128)S(1)} %fusion.19, f32[3,8,64,256]{3,2,1,0:T(8,128)S(1)} %multiply_select_fusion), kind=kOutput, calls=%fused_computation.15 | convolution fusion | flops 102041344 | bytes 3545088 | tf_op jit(solution)/shard_map/bnhqk,bnkhd->bnqhd/dot_general | solution.py:36
  118.4 1.3 %copy.9 = bf16[1,3,64,8,128]{4,3,2,1,0:T(8,128)(2,1)S(1)} copy(bf16[1,3,64,8,128]{4,2,3,1,0:T(8,128)(2,1)} %fusion.12) | data formatting | bytes 786432 | tf_op jit(solution)/shard_map/convert_element_type | solution.py:39
  119.6 0.2 reshape.104
  119.8 0.8 slice.22
  (7 shorter events, 0.0 us)
Async XLA Ops:
  0.0 11.6 %copy-start = (bf16[896,1024]{1,0:T(8,128)(2,1)S(1)}, bf16[896,1024]{1,0:T(8,128)(2,1)}, u32[]{:S(2)}) copy-start(bf16[896,1024]{1,0:T(8,128)(2,1)} %param.8) | copy-start | bytes 5505028
  1.1 104.2 %collective-permute-start = (bf16[1,1,2,64,896]{4,3,2,1,0:T(8,128)(2,1)S(1)}, bf16[1,1,2,64,896]{4,3,2,1,0:T(8,128)(2,1)S(1)}, u32[]{:S(2)}, u32[]{:S(2)}) collective-permute-start(bf16[1,1,2,64,896]{4,3,2,1,0:T(8,128)(2,1)S(1)} %slice.15), channel_id=1, source_target_pairs={{0,2},{2,4},{4,6},{6,8},{8,10},{10,12},{12,14},{14,16},{16,18},{18... | collective-permute-start | bytes 688136 | tf_op jit(solution)/shard_map/ppermute | solution.py:15
  4.9 100.3 %collective-permute-start.1 = (s32[1,1,2]{2,1,0:T(1,128)S(1)}, s32[1,1,2]{2,1,0:T(1,128)S(1)}, u32[]{:S(2)}, u32[]{:S(2)}) collective-permute-start(s32[1,1,2]{2,1,0:T(1,128)S(1)} %slice.17), channel_id=1, source_target_pairs={{0,2},{2,4},{4,6},{6,8},{8,10},{10,12},{12,14},{14,16},{16,18},{18... | collective-permute-start | bytes 32 | tf_op jit(solution)/shard_map/ppermute | solution.py:15
  11.6 1.5 %copy-start.3 = (bf16[896,1024]{1,0:T(8,128)(2,1)S(1)}, bf16[896,1024]{1,0:T(8,128)(2,1)}, u32[]{:S(2)}) copy-start(bf16[896,1024]{1,0:T(8,128)(2,1)} %param.9) | copy-start | bytes 5505028
  13.1 1.4 %copy-start.1 = (bf16[1,128,1024]{2,1,0:T(8,128)(2,1)S(1)}, bf16[1,128,1024]{2,1,0:T(8,128)(2,1)}, u32[]{:S(2)}) copy-start(bf16[1,128,1024]{2,1,0:T(8,128)(2,1)} %param.5) | copy-start | bytes 786436
  13.1 92.2 %copy-start.2 = (s32[1,2,2]{2,1,0:T(2,128)S(1)}, s32[1,2,2]{2,1,0:T(2,128)}, u32[]{:S(2)}) copy-start(s32[1,2,2]{2,1,0:T(2,128)} %param.7) | copy-start | bytes 52

commit v2 on v1

v2 whole, which is shorter than its diff:
```python
import jax
import jax.numpy as jnp
from jax import lax
from jax.experimental import pallas as pl
from jax.experimental.pallas import tpu as pltpu
from jax.sharding import PartitionSpec as P

HEAD_DIM = 128
GROUP_LEN = 64
MASK_FILL = -1e30
MESH_ID = pl.DeviceIdType.MESH

X, Z, HALF = 4, 32, 16
COLUMN_PIECES = {3: 2, 0: 2, 2: 2, 1: 2}
LEGS = (4, 4, 4, 4)
PIECE_ROWS = 8


def piece_table():
    table, at = {}, 0
    most = max(COLUMN_PIECES.values())
    for j in range(most):
        for column, count in COLUMN_PIECES.items():
            if j < count:
                for way in (0, 1):
                    table[column, way, j] = at
                    at += 1
    return table


PIECES = piece_table()
N_PIECES = len(PIECES)
MOST = max(COLUMN_PIECES.values())
N_LEGS = len(LEGS)
SIGN = (1, -1)


def kernel(
    q_hbm, enc_hbm, len_hbm, kw_hbm, vw_hbm, out_ref,
    q_ref, kw_ref, vw_ref, len_ref, prev_len, rows_ref, prev_ref, keys_ref, vals_ref, own_out,
    relay, len_relay,
    in_sem, out_sem, relay_sem, forward_sem, prev_sem, swap_send, swap_recv,
    len_send, len_recv, own_send, own_recv,
):
    seq, fsdp, core = lax.axis_index("seq"), lax.axis_index("fsdp"), lax.axis_index("grp")
    x, y = lax.rem(fsdp, X), lax.div(seq, HALF)
    z = lax.rem(seq, HALF) + HALF * lax.div(fsdp, X)
    other = 1 - core

    def device(to_x, to_y, to_z, to_core):
        return (to_y * HALF + lax.rem(to_z, HALF), lax.div(to_z, HALF) * X + to_x, to_core)

    def wrap(at):
        return lax.rem(at + 2 * Z, Z)

    def target_of(origin):
        return jnp.where(origin < HALF, origin + HALF, origin - (HALF - 1))

    def origin_of(target):
        return jnp.where(target < HALF, target + (HALF - 1), target - HALF)

    sibling = device(x, y, z, other)
    reached = [sum(LEGS[:leg]) for leg in range(N_LEGS + 1)]
    last_z = (z == Z - 1)
    crosses_y = last_z & (y < X - 1)
    has_prev = (x > 0) | (z > 0) | (y > 0)
    columns = list(COLUMN_PIECES)
    far = reached[N_LEGS - 1]

    def remote(src, dst, send, recv, to):
        return pltpu.make_async_remote_copy(
            src_ref=src, dst_ref=dst, send_sem=send, recv_sem=recv, device_id=to, device_id_type=MESH_ID
        )

    def arrived(dst, recv):
        remote(dst, dst, own_send, recv, sibling).wait_recv()

    def left(src, send):
        remote(src, src, send, own_recv, sibling).wait_send()

    barrier = pltpu.get_barrier_semaphore()

    def greet(who):
        pl.semaphore_signal(barrier, 1, device_id=who, device_id_type=MESH_ID)

    greet(sibling)

    @pl.when(x > 0)
    def _():
        greet(device(x - 1, y, z, core))

    for column in columns:
        if column != X - 1:

            @pl.when(x == column)
            def _():
                greet(device(X - 1, y, z, core))

    on_column = (x == columns[0])
    for column in columns[1:]:
        on_column = on_column | (x == column)

    @pl.when(on_column)
    def _():
        for way in (0, 1):
            greet(device(x, y, wrap(z - SIGN[way] * LEGS[0]), core))

    @pl.when((x == 0) & (z > 0))
    def _():
        for column in columns:
            for way in (0, 1):
                greet(device(column, y, wrap(origin_of(z) + SIGN[way] * far), core))

    @pl.when((x == 0) & (z == 0) & (y > 0))
    def _():
        for column in columns:
            greet(device(column, y - 1, Z - 1, core))

    rows_in = pltpu.make_async_copy(enc_hbm.at[0], rows_ref.at[core], in_sem.at[0])
    kw_in = pltpu.make_async_copy(kw_hbm, kw_ref, in_sem.at[1])
    vw_in = pltpu.make_async_copy(vw_hbm, vw_ref, in_sem.at[2])
    q_in = pltpu.make_async_copy(q_hbm.at[0], q_ref, in_sem.at[3])
    len_in = pltpu.make_async_copy(len_hbm.at[0], len_ref, in_sem.at[4])
    for copy in (rows_in, len_in, kw_in, vw_in, q_in):
        copy.start()

    def one(condition, count=1):
        return jnp.where(condition, count, 0)

    peers = 1 + one(x < X - 1) + one(x == X - 1, len(columns) - 1)
    column_peers = 2 + one(crosses_y)
    for way in (0, 1):
        column_peers = column_peers + one(wrap(z - SIGN[way] * far) != Z - 1)
    pl.semaphore_wait(barrier, peers + jnp.where(on_column, column_peers, 0))

    def last_rows(piece):
        at = piece * PIECE_ROWS
        return rows_ref.at[core, 1, at // GROUP_LEN, pl.ds(at % GROUP_LEN, PIECE_ROWS)]

    def prev_rows(half, piece):
        return prev_ref.at[half, pl.ds(piece * PIECE_ROWS, PIECE_ROWS)]

    def to_prev(piece, src, send, to):
        return remote(src, prev_rows(core, piece), send, prev_sem.at[piece], to)

    def relay_at(stage, way, j):
        return relay.at[stage, way, pl.ds(j * PIECE_ROWS, PIECE_ROWS)]

    def lens_to_prev(src, send, to):
        return remote(src, prev_len, send, len_recv.at[N_LEGS], to)

    rows_in.wait()
    len_in.wait()
    own_swap = remote(rows_ref.at[core], rows_ref.at[core], own_send, own_recv, sibling)

    @pl.when(x == X - 1)
    def _():
        for (column, way, j), piece in PIECES.items():
            src, send = last_rows(piece), out_sem.at[piece]
            if column != X - 1:

                @pl.when((z < Z - 1) | (y < X - 1))
                def _():
                    remote(
                        src, relay_at(0, way, j), send, relay_sem.at[0, way, j], device(column, y, z, core)
                    ).start()

            else:

                @pl.when(z < Z - 1)
                def _():
                    remote(
                        src, relay_at(1, way, j), send, relay_sem.at[1, way, j],
                        device(column, y, wrap(z + SIGN[way] * LEGS[0]), core),
                    ).start()

                @pl.when(crosses_y)
                def _():
                    to_prev(piece, src, send, device(0, y + 1, 0, core)).start()

        @pl.when(z < Z - 1)
        def _():
            remote(
                len_ref, len_relay.at[1], len_send.at[0], len_recv.at[1],
                device(X - 1, y, wrap(z + LEGS[0]), core),
            ).start()

        @pl.when(crosses_y)
        def _():
            lens_to_prev(len_ref, len_send.at[0], device(0, y + 1, 0, core)).start()

    @pl.when(x < X - 1)
    def _():
        to = device(x + 1, y, z, core)
        for piece in range(N_PIECES):
            to_prev(piece, last_rows(piece), out_sem.at[piece], to).start()
        lens_to_prev(len_ref, len_send.at[0], to).start()

    own_swap.start()

    row_in_keys = lax.broadcasted_iota(jnp.int32, (1, 4 * GROUP_LEN), 1)
    key_position = (row_in_keys // (2 * GROUP_LEN)) * GROUP_LEN + row_in_keys % GROUP_LEN
    key_neighbour = (row_in_keys // GROUP_LEN) % 2

    def key_live(lens):
        length = jnp.where(
            key_neighbour == 0,
            jnp.broadcast_to(lens[:, 0:1], row_in_keys.shape),
            jnp.broadcast_to(lens[:, 1:2], row_in_keys.shape),
        )
        return key_position < length

    def project(rows, slot):
        def columns_of(tile, carry):
            at = pl.ds(pl.multiple_of(tile * 256, 256), 256)
            keys_ref[slot, :, at] = jnp.dot(
                rows, kw_ref[:, at], preferred_element_type=jnp.float32
            ).astype(jnp.bfloat16)
            vals_ref[slot, :, at] = jnp.dot(
                rows, vw_ref[:, at], preferred_element_type=jnp.float32
            ).astype(jnp.bfloat16)
            return carry

        lax.fori_loop(0, kw_ref.shape[1] // 256, columns_of, 0)

    def attend(head, first, count, slot, live):
        at = pl.ds(head * HEAD_DIM, HEAD_DIM)
        scores = lax.dot_general(
            q_ref[first : first + count, at], keys_ref[slot, :, at],
            (((1,), (1,)), ((), ())), preferred_element_type=jnp.float32,
        ) * HEAD_DIM ** (-0.5)
        scores = jnp.where(live, scores, MASK_FILL)
        weights = jnp.exp(scores - jnp.max(scores, axis=-1, keepdims=True))
        attention = (weights / jnp.sum(weights, axis=-1, keepdims=True)).astype(jnp.bfloat16)
        return jnp.dot(attention, vals_ref[slot, :, at], preferred_element_type=jnp.float32).astype(
            jnp.bfloat16
        )

    n_heads = q_ref.shape[1] // HEAD_DIM

    def own_rows(group):
        return rows_ref[:, group].reshape(4 * GROUP_LEN, rows_ref.shape[-1])

    def step_own_project(group):
        if group == 0:
            kw_in.wait()
            vw_in.wait()
            arrived(rows_ref.at[other], own_recv)
        project(own_rows(group), group)

    def step_own_attend():
        q_in.wait()
        lens = len_ref[...]
        live0, live1 = key_live(lens[0:1]), key_live(lens[1:2])
        row = lax.broadcasted_iota(jnp.int32, (2 * GROUP_LEN, HEAD_DIM), 0)
        for head in range(n_heads):
            at = pl.ds(head * HEAD_DIM, HEAD_DIM)
            mid = attend(head, 0, 2 * GROUP_LEN, 0, live0)
            end = attend(head, GROUP_LEN, GROUP_LEN, 1, live1)
            end = jnp.concatenate([mid[:GROUP_LEN], end], axis=0)
            merged = jnp.where(row < 2 * GROUP_LEN - 1, mid, end)
            own_out[:, at] = merged

    def own_work(step):
        if step == 0:
            step_own_project(0)
        elif step == 1:
            step_own_project(1)
        elif step == 2:
            step_own_attend()

    def forward(stage, column):
        for j in range(COLUMN_PIECES[column]):
            for way in (0, 1):
                piece = PIECES[column, way, j]
                origin = wrap(z - SIGN[way] * reached[stage])
                src, send = relay_at(stage, way, j), forward_sem.at[stage, way, j]
                onward = origin != Z - 1

                @pl.when(onward)
                def _():
                    arrived(src, relay_sem.at[stage, way, j])
                    if stage < N_LEGS - 1:
                        remote(
                            src, relay_at(stage + 1, way, j), send, relay_sem.at[stage + 1, way, j],
                            device(column, y, wrap(z + SIGN[way] * LEGS[stage]), core),
                        ).start()
                    else:
                        to_prev(piece, src, send, device(0, y, target_of(origin), core)).start()

                if stage == 0:

                    @pl.when(crosses_y)
                    def _():
                        arrived(src, relay_sem.at[stage, way, j])
                        to_prev(piece, src, send, device(0, y + 1, 0, core)).start()

        if column == X - 1:
            origin = wrap(z - reached[stage])

            @pl.when(origin != Z - 1)
            def _():
                arrived(len_relay.at[stage], len_recv.at[stage])
                if stage < N_LEGS - 1:
                    remote(
                        len_relay.at[stage], len_relay.at[stage + 1], len_send.at[stage],
                        len_recv.at[stage + 1], device(column, y, wrap(z + LEGS[stage]), core),
                    ).start()
                else:
                    lens_to_prev(
                        len_relay.at[stage], len_send.at[stage], device(0, y, target_of(origin), core)
                    ).start()

    def settle(stage, column):
        for j in range(COLUMN_PIECES[column]):
            for way in (0, 1):
                origin = wrap(z - SIGN[way] * reached[stage])
                sent = origin != Z - 1
                if stage == 0:
                    sent = sent | crosses_y

                @pl.when(sent)
                def _():
                    left(relay_at(stage, way, j), forward_sem.at[stage, way, j])

        if column == X - 1:

            @pl.when(wrap(z - reached[stage]) != Z - 1)
            def _():
                left(len_relay.at[stage], len_send.at[stage])

    for stage in range(N_LEGS):
        for column in columns:
            if stage > 0 or column != X - 1:

                @pl.when(x == column)
                def _():
                    forward(stage, column)

        own_work(stage)

    @pl.when(has_prev)
    def _():
        for piece in range(N_PIECES):
            arrived(prev_rows(core, piece), prev_sem.at[piece])
            remote(
                prev_rows(core, piece), prev_rows(core, piece), swap_send.at[piece], swap_recv.at[piece], sibling
            ).start()
        arrived(prev_len, len_recv.at[N_LEGS])
        for piece in range(N_PIECES):
            arrived(prev_rows(other, piece), swap_recv.at[piece])

        project(prev_ref[...].reshape(4 * GROUP_LEN, prev_ref.shape[-1]), 2)
        live = key_live(prev_len[1:2])
        row = lax.broadcasted_iota(jnp.int32, (GROUP_LEN, HEAD_DIM), 0)
        for head in range(n_heads):
            at = pl.ds(head * HEAD_DIM, HEAD_DIM)
            first = attend(head, 0, GROUP_LEN, 2, live)
            out_ref[0, :GROUP_LEN, at] = jnp.where(row < GROUP_LEN - 1, first, own_out[:GROUP_LEN, at])

    @pl.when(jnp.logical_not(has_prev))
    def _():
        row = lax.broadcasted_iota(jnp.int32, (GROUP_LEN, own_out.shape[1]), 0)
        out_ref[0, :GROUP_LEN] = jnp.where(row < GROUP_LEN - 1, jnp.zeros_like(row, jnp.bfloat16), own_out[:GROUP_LEN])

    out_ref[0, GROUP_LEN:] = own_out[GROUP_LEN:]

    left(rows_ref.at[core], own_send)

    @pl.when((x < X - 1) | (z < Z - 1) | (y < X - 1))
    def _():
        for piece in range(N_PIECES):
            left(last_rows(piece), out_sem.at[piece])
        left(len_ref, len_send.at[0])

    for stage in range(N_LEGS):
        for column in columns:
            if stage > 0 or column != X - 1:

                @pl.when(x == column)
                def _():
                    settle(stage, column)

    @pl.when(has_prev)
    def _():
        for piece in range(N_PIECES):
            left(prev_rows(core, piece), swap_send.at[piece])


def shards(queries, encodings, neighbour_lengths, key_weight, value_weight):
    _, group_count, neighbours, half_rows, enc_width = encodings.shape
    tok_count, col_count = queries.shape[1:]
    bf16 = jnp.bfloat16
    anywhere = pl.BlockSpec(memory_space=pl.ANY)
    dma = pltpu.SemaphoreType.DMA
    return pl.pallas_call(
        kernel,
        out_shape=jax.ShapeDtypeStruct(queries.shape, bf16),
        in_specs=[anywhere] * 5,
        out_specs=pl.BlockSpec(memory_space=pltpu.VMEM),
        scratch_shapes=[
            pltpu.VMEM((tok_count, col_count), bf16),
            pltpu.VMEM(key_weight.shape, bf16),
            pltpu.VMEM(value_weight.shape, bf16),
            pltpu.VMEM((group_count, neighbours), jnp.int32),
            pltpu.VMEM((group_count, neighbours), jnp.int32),
            pltpu.VMEM((2, group_count, neighbours, half_rows, enc_width), bf16),
            pltpu.VMEM((2, neighbours * half_rows, enc_width), bf16),
            pltpu.VMEM((3, 2 * neighbours * half_rows, col_count), bf16),
            pltpu.VMEM((3, 2 * neighbours * half_rows, col_count), bf16),
            pltpu.VMEM((tok_count, col_count), bf16),
            pltpu.VMEM((N_LEGS, 2, MOST * PIECE_ROWS, enc_width), bf16),
            pltpu.VMEM((N_LEGS, group_count, neighbours), jnp.int32),
            dma((5,)),
            dma((N_PIECES,)),
            dma((N_LEGS, 2, MOST)),
            dma((N_LEGS, 2, MOST)),
            dma((N_PIECES,)),
            dma((N_PIECES,)),
            dma((N_PIECES,)),
            dma((N_LEGS,)),
            dma((N_LEGS + 1,)),
            dma,
            dma,
        ],
        compiler_params=pltpu.CompilerParams(
            collective_id=0, has_side_effects=True, vmem_limit_bytes=56 * 2**20
        ),
        name="attend_neighbours",
    )(queries, encodings, neighbour_lengths, key_weight, value_weight)


def solution(mesh):
    placed = (
        P(None, ("seq", "fsdp"), "grp"),
        P(None, ("seq", "fsdp"), None, "grp", None),
        P(None, ("seq", "fsdp"), None),
        P(None, "grp"),
        P(None, "grp"),
    )
    return jax.shard_map(
        shards,
        mesh=mesh,
        in_specs=placed,
        out_specs=P(None, ("seq", "fsdp"), "grp"),
        check_vma=False,
    )
```

time: 121 us -> 54.1 us (0.45)
  the two profiles are of different devices: /device:TPU:33 before, /device:TPU:57 now
where the time goes in v2:
time: 54.1 us; the launch traced here: 53.9 us
  Pallas kernels  52.2 us (96%)
  local copies, waits for them, and re-layouts  1.67 us (3%)
    pallas_call x1, Pallas kernels, shards(): pl.pallas_call(kernel, out_shape=jax.ShapeDtypeStruct(queries.shape, bf16...  52.2 us
    unnamed x1, local copies, waits for them, and re-layouts  1.67 us

profile of v2, /device:TPU:57, one launch (start us, length us, event | category | flops | bytes accessed | tf_op | source)
XLA Modules:
  0.0 53.9 jit_solution(13640368135522148066)
XLA Ops:
  0.0 52.2 %attend_neighbours.1 = bf16[1,128,1024]{2,1,0:T(8,128)(2,1)} custom-call(bf16[1,128,1024]{2,1,0:T(8,128)(2,1)} %q_hbm.1, bf16[1,2,2,64,896]{4,3,2,1,0:T(8,128)(2,1)} %enc_hbm.1, s32[1,2,2]{2,1,0:T(2,128)} %len_hbm.1, bf16[896,1024]{1,0:T(8,128)(2,1)} %kw_hbm.1, bf16[896,1024]{1,0:T(8,128)(2,1)} %vw_hbm.1), custom_call_target="tpu_custom_call" | custom-call | tf_op jit(solution)/shard_map/attend_neighbours/pallas_call | solution.py:396
  52.2 1.7 %copy.7 = bf16[1,128,1024]{2,1,0:T(8,128)(2,1)} copy(bf16[1,128,1024]{2,1,0:T(8,128)(2,1)} %attend_neighbours.1) | data formatting | bytes 524288

commit v3 on v2

v3 whole, which is shorter than its diff:
```python
import jax
import jax.numpy as jnp
from jax import lax
from jax.experimental import pallas as pl
from jax.experimental.pallas import tpu as pltpu
from jax.sharding import PartitionSpec as P

HEAD_DIM = 128
GROUP_LEN = 64
MASK_FILL = -1e30
MESH_ID = pl.DeviceIdType.MESH

X, Z, HALF = 4, 32, 16
COLUMN_PIECES = {3: 4, 0: 4, 2: 4, 1: 4}
HOPS = (((0, 8, 8), (18, 22, 2)), ((0, 4, -4), (4, 8, 8), (18, 22, 2)))
PIECE_ROWS = 8
PIECES = {}
for _j in range(max(COLUMN_PIECES.values())):
    for _column, _count in COLUMN_PIECES.items():
        if _j < _count:
            PIECES[_column, _j] = len(PIECES)
N_PIECES = len(PIECES)
MOST = max(COLUMN_PIECES.values())


def kernel(
    q_hbm, enc_hbm, len_hbm, kw_hbm, vw_hbm, out_ref,
    q_ref, kw_ref, vw_ref, len_ref, prev_len, rows_ref, prev_ref, keys_ref, vals_ref, own_out,
    relay, len_relay,
    in_sem, out_sem, relay_sem, forward_sem, prev_sem, swap_send, swap_recv,
    len_send, len_recv, own_send, own_recv,
):
    seq, fsdp, core = lax.axis_index("seq"), lax.axis_index("fsdp"), lax.axis_index("grp")
    x, y = lax.rem(fsdp, X), lax.div(seq, HALF)
    z = lax.rem(seq, HALF) + HALF * lax.div(fsdp, X)
    other = 1 - core

    def device(to_x, to_y, to_z, to_core):
        return (to_y * HALF + lax.rem(to_z, HALF), lax.div(to_z, HALF) * X + to_x, to_core)

    sibling = device(x, y, z, other)
    last_z = (z == Z - 1)
    crosses_y = last_z & (y < X - 1)
    has_prev = (x > 0) | (z > 0) | (y > 0)
    columns = list(COLUMN_PIECES)

    def wrap(at):
        return lax.rem(at + Z, Z)

    def hop_of(origin, way):
        hop = jnp.zeros_like(origin)
        for first, end, by in HOPS[way]:
            hop = jnp.where((origin >= first) & (origin < end), by, hop)
        return hop

    def passed_by(way):
        origin = jnp.full_like(z, Z)
        for first, end, by in HOPS[way]:
            at = wrap(z - by)
            origin = jnp.where((at >= first) & (at < end), at, origin)
        return origin

    hops = [hop_of(z, way) for way in (0, 1)]
    direct = [(hop == 0) & (z < Z - 1) for hop in hops]
    loops = [hop != 0 for hop in hops]
    onward = [wrap(z + hop) for hop in hops]
    passed = [passed_by(way) for way in (0, 1)]
    passes = [origin < Z for origin in passed]

    def target_of(origin):
        return jnp.where(origin < HALF, origin + HALF, origin - (HALF - 1))

    def origin_of(target):
        return jnp.where(target < HALF, target + (HALF - 1), target - HALF)

    def remote(src, dst, send, recv, to):
        return pltpu.make_async_remote_copy(
            src_ref=src, dst_ref=dst, send_sem=send, recv_sem=recv, device_id=to, device_id_type=MESH_ID
        )

    def arrived(dst, recv):
        remote(dst, dst, own_send, recv, sibling).wait_recv()

    def left(src, send):
        remote(src, src, send, own_recv, sibling).wait_send()

    barrier = pltpu.get_barrier_semaphore()

    def greet(who):
        pl.semaphore_signal(barrier, 1, device_id=who, device_id_type=MESH_ID)

    greet(sibling)

    @pl.when(x > 0)
    def _():
        greet(device(x - 1, y, z, core))

    for column in columns:
        if column != X - 1:

            @pl.when(x == column)
            def _():
                greet(device(X - 1, y, z, core))

    on_column = (x == columns[0])
    for column in columns[1:]:
        on_column = on_column | (x == column)

    for way in (0, 1):

        @pl.when(on_column & passes[way])
        def _():
            greet(device(x, y, passed[way], core))

    @pl.when((x == 0) & (z > 0))
    def _():
        origin = origin_of(z)
        for column in columns:
            for way in (0, 1):
                greet(device(column, y, wrap(origin + hop_of(origin, way)), core))

    @pl.when((x == 0) & (z == 0) & (y > 0))
    def _():
        for column in columns:
            greet(device(column, y - 1, Z - 1, core))

    rows_in = pltpu.make_async_copy(enc_hbm.at[0], rows_ref.at[core], in_sem.at[0])
    kw_in = pltpu.make_async_copy(kw_hbm, kw_ref, in_sem.at[1])
    vw_in = pltpu.make_async_copy(vw_hbm, vw_ref, in_sem.at[2])
    q_in = pltpu.make_async_copy(q_hbm.at[0], q_ref, in_sem.at[3])
    len_in = pltpu.make_async_copy(len_hbm.at[0], len_ref, in_sem.at[4])
    for copy in (rows_in, len_in, kw_in, vw_in, q_in):
        copy.start()

    def one(condition, count=1):
        return jnp.where(condition, count, 0)

    peers = 1 + one(x < X - 1) + one(x == X - 1, len(columns) - 1)
    column_peers = one(crosses_y)
    for way in (0, 1):
        column_peers = column_peers + one(z < Z - 1) + one(passes[way])
    pl.semaphore_wait(barrier, peers + jnp.where(on_column, column_peers, 0))

    def last_rows(piece):
        at = piece * PIECE_ROWS
        return rows_ref.at[core, 1, at // GROUP_LEN, pl.ds(at % GROUP_LEN, PIECE_ROWS)]

    def prev_rows(half, piece):
        return prev_ref.at[half, pl.ds(piece * PIECE_ROWS, PIECE_ROWS)]

    def to_prev(piece, src, send, to):
        return remote(src, prev_rows(core, piece), send, prev_sem.at[piece], to)

    def relay_at(stage, j):
        return relay.at[stage, pl.ds(j * PIECE_ROWS, PIECE_ROWS)]

    def lens_to_prev(src, send, to):
        return remote(src, prev_len, send, len_recv.at[0], to)

    rows_in.wait()
    len_in.wait()
    own_swap = remote(rows_ref.at[core], rows_ref.at[core], own_send, own_recv, sibling)

    @pl.when(x == X - 1)
    def _():
        for (column, j), piece in PIECES.items():
            src, send, way = last_rows(piece), out_sem.at[piece], j % 2
            if column != X - 1:

                @pl.when((z < Z - 1) | (y < X - 1))
                def _():
                    to = device(column, y, z, core)
                    remote(src, relay_at(0, j), send, relay_sem.at[0, j], to).start()

            else:

                @pl.when(direct[way])
                def _():
                    to_prev(piece, src, send, device(0, y, target_of(z), core)).start()

                @pl.when(loops[way])
                def _():
                    to = device(column, y, onward[way], core)
                    remote(src, relay_at(1, j), send, relay_sem.at[1, j], to).start()

                @pl.when(crosses_y)
                def _():
                    to_prev(piece, src, send, device(0, y + 1, 0, core)).start()

        @pl.when(direct[0])
        def _():
            lens_to_prev(len_ref, len_send.at[0], device(0, y, target_of(z), core)).start()

        @pl.when(loops[0])
        def _():
            to = device(X - 1, y, onward[0], core)
            remote(len_ref, len_relay, len_send.at[0], len_recv.at[1], to).start()

        @pl.when(crosses_y)
        def _():
            lens_to_prev(len_ref, len_send.at[0], device(0, y + 1, 0, core)).start()

    own_swap.start()

    row_in_keys = lax.broadcasted_iota(jnp.int32, (1, 4 * GROUP_LEN), 1)
    key_position = (row_in_keys // (2 * GROUP_LEN)) * GROUP_LEN + row_in_keys % GROUP_LEN
    key_neighbour = (row_in_keys // GROUP_LEN) % 2

    def key_live(lens):
        length = jnp.where(
            key_neighbour == 0,
            jnp.broadcast_to(lens[:, 0:1], row_in_keys.shape),
            jnp.broadcast_to(lens[:, 1:2], row_in_keys.shape),
        )
        return key_position < length

    def project(rows, slot, at_row=0):
        into = pl.ds(at_row, rows.shape[0])

        def columns_of(tile, carry):
            at = pl.ds(pl.multiple_of(tile * 256, 256), 256)
            keys_ref[slot, into, at] = jnp.dot(
                rows, kw_ref[:, at], preferred_element_type=jnp.float32
            ).astype(jnp.bfloat16)
            vals_ref[slot, into, at] = jnp.dot(
                rows, vw_ref[:, at], preferred_element_type=jnp.float32
            ).astype(jnp.bfloat16)
            return carry

        lax.fori_loop(0, kw_ref.shape[1] // 256, columns_of, 0)

    def attend(first, count, slot, live):
        heads = [pl.ds(head * HEAD_DIM, HEAD_DIM) for head in range(q_ref.shape[1] // HEAD_DIM)]
        scores = [
            lax.dot_general(
                q_ref[first : first + count, at], keys_ref[slot, :, at],
                (((1,), (1,)), ((), ())), preferred_element_type=jnp.float32,
            )
            for at in heads
        ]
        scores = [jnp.where(live, each * HEAD_DIM ** (-0.5), MASK_FILL) for each in scores]
        most = [jnp.max(each, axis=-1, keepdims=True) for each in scores]
        weights = [jnp.exp(each - top) for each, top in zip(scores, most)]
        totals = [jnp.sum(each, axis=-1, keepdims=True) for each in weights]
        attention = [(each / total).astype(jnp.bfloat16) for each, total in zip(weights, totals)]
        return [
            jnp.dot(each, vals_ref[slot, :, at], preferred_element_type=jnp.float32).astype(jnp.bfloat16)
            for each, at in zip(attention, heads)
        ]

    def own_rows(group):
        return rows_ref[:, group].reshape(4 * GROUP_LEN, rows_ref.shape[-1])

    def step_own_project(group):
        if group == 0:
            kw_in.wait()
            vw_in.wait()
            arrived(rows_ref.at[other], own_recv)
        project(own_rows(group), group)

    def step_own_attend():
        q_in.wait()
        lens = len_ref[...]
        live0, live1 = key_live(lens[0:1]), key_live(lens[1:2])
        row = lax.broadcasted_iota(jnp.int32, (16, HEAD_DIM), 0)
        middle = attend(GROUP_LEN - 16, GROUP_LEN + 16, 0, live0)
        end = attend(2 * GROUP_LEN - 16, 16, 1, live1)
        for head, (mid, last) in enumerate(zip(middle, end)):
            at = pl.ds(head * HEAD_DIM, HEAD_DIM)
            own_out[GROUP_LEN - 16 : 2 * GROUP_LEN - 16, at] = mid[:GROUP_LEN]
            own_out[2 * GROUP_LEN - 16 :, at] = jnp.where(row < 15, mid[GROUP_LEN:], last)

    def own_work(step):
        if step == 0:
            step_own_project(0)
        elif step == 1:
            step_own_project(1)
        elif step == 2:
            step_own_attend()

    def forward(column):
        for j in range(COLUMN_PIECES[column]):
            piece, way = PIECES[column, j], j % 2
            src, send, got = relay_at(0, j), forward_sem.at[0, j], relay_sem.at[0, j]

            @pl.when(direct[way])
            def _():
                arrived(src, got)
                to_prev(piece, src, send, device(0, y, target_of(z), core)).start()

            @pl.when(loops[way])
            def _():
                arrived(src, got)
                to = device(column, y, onward[way], core)
                remote(src, relay_at(1, j), send, relay_sem.at[1, j], to).start()

            @pl.when(crosses_y)
            def _():
                arrived(src, got)
                to_prev(piece, src, send, device(0, y + 1, 0, core)).start()

    def pass_on(column, way):
        to = device(0, y, target_of(passed[way]), core)
        for j in range(way, COLUMN_PIECES[column], 2):
            arrived(relay_at(1, j), relay_sem.at[1, j])
            to_prev(PIECES[column, j], relay_at(1, j), forward_sem.at[1, j], to).start()
        if column == X - 1 and way == 0:
            arrived(len_relay, len_recv.at[1])
            lens_to_prev(len_relay, len_send.at[1], to).start()

    def send_across():
        to = device(x + 1, y, z, core)
        for piece in range(N_PIECES):
            to_prev(piece, last_rows(piece), out_sem.at[piece], to).start()
        lens_to_prev(len_ref, len_send.at[0], to).start()

    @pl.when((x < X - 1) & (z < HALF))
    def _():
        send_across()

    for column in columns:
        if column != X - 1:

            @pl.when(x == column)
            def _():
                forward(column)

    @pl.when((x < X - 1) & (z >= HALF))
    def _():
        send_across()

    for way in (0, 1):
        for column in columns:

            @pl.when((x == column) & passes[way])
            def _():
                pass_on(column, way)

    for step in range(3):
        own_work(step)

    @pl.when(has_prev)
    def _():
        for piece in range(N_PIECES):
            arrived(prev_rows(core, piece), prev_sem.at[piece])
            remote(
                prev_rows(core, piece), prev_rows(core, piece), swap_send.at[piece], swap_recv.at[piece], sibling
            ).start()
        arrived(prev_len, len_recv.at[0])
        half = prev_ref.shape[1]
        project(prev_ref[core], 2, pl.multiple_of(core * half, half))
        for piece in range(N_PIECES):
            arrived(prev_rows(other, piece), swap_recv.at[piece])
        project(prev_ref[other], 2, pl.multiple_of(other * half, half))
        live = key_live(prev_len[1:2])
        row = lax.broadcasted_iota(jnp.int32, (16, HEAD_DIM), 0)
        edge = pl.ds(GROUP_LEN - 16, 16)
        for head, first in enumerate(attend(0, GROUP_LEN, 2, live)):
            at = pl.ds(head * HEAD_DIM, HEAD_DIM)
            out_ref[0, : GROUP_LEN - 16, at] = first[: GROUP_LEN - 16]
            out_ref[0, edge, at] = jnp.where(row < 15, first[GROUP_LEN - 16 :], own_out[edge, at])

    @pl.when(jnp.logical_not(has_prev))
    def _():
        row = lax.broadcasted_iota(jnp.int32, (16, own_out.shape[1]), 0)
        edge = pl.ds(GROUP_LEN - 16, 16)
        out_ref[0, : GROUP_LEN - 16] = jnp.zeros((GROUP_LEN - 16, own_out.shape[1]), jnp.bfloat16)
        out_ref[0, edge] = jnp.where(row < 15, jnp.zeros_like(row, jnp.bfloat16), own_out[edge])

    out_ref[0, GROUP_LEN:] = own_out[GROUP_LEN:]

    left(rows_ref.at[core], own_send)

    @pl.when((x < X - 1) | (z < Z - 1) | (y < X - 1))
    def _():
        for piece in range(N_PIECES):
            left(last_rows(piece), out_sem.at[piece])
        left(len_ref, len_send.at[0])

    for column in columns:
        if column != X - 1:

            @pl.when((x == column) & ((z < Z - 1) | (y < X - 1)))
            def _():
                for j in range(COLUMN_PIECES[column]):
                    left(relay_at(0, j), forward_sem.at[0, j])

        for way in (0, 1):

            @pl.when((x == column) & passes[way])
            def _():
                for j in range(way, COLUMN_PIECES[column], 2):
                    left(relay_at(1, j), forward_sem.at[1, j])
                if column == X - 1 and way == 0:
                    left(len_relay, len_send.at[1])

    @pl.when(has_prev)
    def _():
        for piece in range(N_PIECES):
            left(prev_rows(core, piece), swap_send.at[piece])


def shards(queries, encodings, neighbour_lengths, key_weight, value_weight):
    _, group_count, neighbours, half_rows, enc_width = encodings.shape
    tok_count, col_count = queries.shape[1:]
    bf16 = jnp.bfloat16
    anywhere = pl.BlockSpec(memory_space=pl.ANY)
    dma = pltpu.SemaphoreType.DMA
    return pl.pallas_call(
        kernel,
        out_shape=pltpu.VMEM(queries.shape, bf16),
        in_specs=[anywhere] * 5,
        out_specs=pl.BlockSpec(memory_space=pltpu.VMEM),
        scratch_shapes=[
            pltpu.VMEM((tok_count, col_count), bf16),
            pltpu.VMEM(key_weight.shape, bf16),
            pltpu.VMEM(value_weight.shape, bf16),
            pltpu.VMEM((group_count, neighbours), jnp.int32),
            pltpu.VMEM((group_count, neighbours), jnp.int32),
            pltpu.VMEM((2, group_count, neighbours, half_rows, enc_width), bf16),
            pltpu.VMEM((2, neighbours * half_rows, enc_width), bf16),
            pltpu.VMEM((3, 2 * neighbours * half_rows, col_count), bf16),
            pltpu.VMEM((3, 2 * neighbours * half_rows, col_count), bf16),
            pltpu.VMEM((tok_count, col_count), bf16),
            pltpu.VMEM((2, MOST * PIECE_ROWS, enc_width), bf16),
            pltpu.VMEM((group_count, neighbours), jnp.int32),
            dma((5,)),
            dma((N_PIECES,)),
            dma((2, MOST)),
            dma((2, MOST)),
            dma((N_PIECES,)),
            dma((N_PIECES,)),
            dma((N_PIECES,)),
            dma((2,)),
            dma((2,)),
            dma,
            dma,
        ],
        compiler_params=pltpu.CompilerParams(
            collective_id=0, has_side_effects=True, vmem_limit_bytes=56 * 2**20
        ),
        name="attend_neighbours",
    )(queries, encodings, neighbour_lengths, key_weight, value_weight)


def solution(mesh):
    placed = (
        P(None, ("seq", "fsdp"), "grp"),
        P(None, ("seq", "fsdp"), None, "grp", None),
        P(None, ("seq", "fsdp"), None),
        P(None, "grp"),
        P(None, "grp"),
    )
    return jax.shard_map(
        shards,
        mesh=mesh,
        in_specs=placed,
        out_specs=P(None, ("seq", "fsdp"), "grp"),
        check_vma=False,
    )
```

time: 54.1 us -> 42.7 us (0.79)
  Pallas kernels: 52.2 us -> 41.8 us
  local copies, waits for them, and re-layouts: 1.67 us -> 0.71 us
    pallas_call x1, Pallas kernels: 52.2 us -> 41.8 us  [shards(): pl.pallas_call(kernel, out_shape=pltpu.VMEM(queries.shape, bf16), in_spec...]
    unnamed x1, local copies, waits for them, and re-layouts: 1.67 us -> 0.71 us
where the time goes in v3:
time: 42.7 us; the launch traced here: 42.5 us
  Pallas kernels  41.8 us (98%)
  local copies, waits for them, and re-layouts  0.71 us (2%)
    pallas_call x1, Pallas kernels, shards(): pl.pallas_call(kernel, out_shape=pltpu.VMEM(queries.shape, bf16), in_spec...  41.8 us

profile of v3, /device:TPU:57, one launch (start us, length us, event | category | flops | bytes accessed | tf_op | source)
XLA Modules:
  0.0 42.5 jit_solution(1055238995487303655)
XLA Ops:
  0.0 41.8 %attend_neighbours.1 = bf16[1,128,1024]{2,1,0:T(8,128)(2,1)S(1)} custom-call(bf16[1,128,1024]{2,1,0:T(8,128)(2,1)} %q_hbm.1, bf16[1,2,2,64,896]{4,3,2,1,0:T(8,128)(2,1)} %enc_hbm.1, s32[1,2,2]{2,1,0:T(2,128)} %len_hbm.1, bf16[896,1024]{1,0:T(8,128)(2,1)} %kw_hbm.1, bf16[896,1024]{1,0:T(8,128)(2,1)} %vw_hbm.1), custom_call_target="tpu_custom_call" | custom-call | tf_op jit(solution)/shard_map/attend_neighbours/pallas_call | solution.py:409
  41.8 0.7 %copy.7 = bf16[1,128,1024]{2,1,0:T(8,128)(2,1)} copy(bf16[1,128,1024]{2,1,0:T(8,128)(2,1)S(1)} %attend_neighbours.1) | data formatting | bytes 524288

commit v4 on v3

--- a/solution.py
+++ b/solution.py
@@ -12,20 +12,20 @@
 
 X, Z, HALF = 4, 32, 16
 COLUMN_PIECES = {3: 4, 0: 4, 2: 4, 1: 4}
-HOPS = (((0, 8, 8), (18, 22, 2)), ((0, 4, -4), (4, 8, 8), (18, 22, 2)))
+HOPS = (((0, 8, 8), (18,26,2)), ((0, 3, -4), (3, 8, 8), (18,26,2)))
 PIECE_ROWS = 8
-PIECES = {}
-for _j in range(max(COLUMN_PIECES.values())):
-    for _column, _count in COLUMN_PIECES.items():
-        if _j < _count:
-            PIECES[_column, _j] = len(PIECES)
+PIECES, SPANS = {}, {}
+for _column, _count in COLUMN_PIECES.items():
+    SPANS[_column] = (len(PIECES), _count)
+    for _j in range(_count):
+        PIECES[_column, _j] = len(PIECES)
 N_PIECES = len(PIECES)
 MOST = max(COLUMN_PIECES.values())
 
 
 def kernel(
     q_hbm, enc_hbm, len_hbm, kw_hbm, vw_hbm, out_ref,
-    q_ref, kw_ref, vw_ref, len_ref, prev_len, rows_ref, prev_ref, keys_ref, vals_ref, own_out,
+    q_ref, kw_ref, vw_ref, len_ref, prev_len, rows_ref, prev_ref, keys_ref, vals_ref, own_edge,
     relay, len_relay,
     in_sem, out_sem, relay_sem, forward_sem, prev_sem, swap_send, swap_recv,
     len_send, len_recv, own_send, own_recv,
@@ -148,6 +148,10 @@
     def prev_rows(half, piece):
         return prev_ref.at[half, pl.ds(piece * PIECE_ROWS, PIECE_ROWS)]
 
+    def span_rows(half, column):
+        first, count = SPANS[column]
+        return prev_ref.at[half, pl.ds(first * PIECE_ROWS, count * PIECE_ROWS)]
+
     def to_prev(piece, src, send, to):
         return remote(src, prev_rows(core, piece), send, prev_sem.at[piece], to)
 
@@ -217,17 +221,14 @@
     def project(rows, slot, at_row=0):
         into = pl.ds(at_row, rows.shape[0])
 
-        def columns_of(tile, carry):
-            at = pl.ds(pl.multiple_of(tile * 256, 256), 256)
+        for tile in range(kw_ref.shape[1] // 256):
+            at = pl.ds(tile * 256, 256)
             keys_ref[slot, into, at] = jnp.dot(
                 rows, kw_ref[:, at], preferred_element_type=jnp.float32
             ).astype(jnp.bfloat16)
             vals_ref[slot, into, at] = jnp.dot(
                 rows, vw_ref[:, at], preferred_element_type=jnp.float32
             ).astype(jnp.bfloat16)
-            return carry
-
-        lax.fori_loop(0, kw_ref.shape[1] // 256, columns_of, 0)
 
     def attend(first, count, slot, live):
         heads = [pl.ds(head * HEAD_DIM, HEAD_DIM) for head in range(q_ref.shape[1] // HEAD_DIM)]
@@ -267,8 +268,9 @@
         end = attend(2 * GROUP_LEN - 16, 16, 1, live1)
         for head, (mid, last) in enumerate(zip(middle, end)):
             at = pl.ds(head * HEAD_DIM, HEAD_DIM)
-            own_out[GROUP_LEN - 16 : 2 * GROUP_LEN - 16, at] = mid[:GROUP_LEN]
-            own_out[2 * GROUP_LEN - 16 :, at] = jnp.where(row < 15, mid[GROUP_LEN:], last)
+            own_edge[:, at] = mid[:16]
+            out_ref[0, GROUP_LEN : 2 * GROUP_LEN - 16, at] = mid[16:GROUP_LEN]
+            out_ref[0, 2 * GROUP_LEN - 16 :, at] = jnp.where(row < 15, mid[GROUP_LEN:], last)
 
     def own_work(step):
         if step == 0:
@@ -339,18 +341,44 @@
     for step in range(3):
         own_work(step)
 
+    left(rows_ref.at[core], own_send)
+
+    @pl.when((x < X - 1) | (z < Z - 1) | (y < X - 1))
+    def _():
+        for piece in range(N_PIECES):
+            left(last_rows(piece), out_sem.at[piece])
+        left(len_ref, len_send.at[0])
+
+    for column in columns:
+        if column != X - 1:
+
+            @pl.when((x == column) & ((z < Z - 1) | (y < X - 1)))
+            def _():
+                for j in range(COLUMN_PIECES[column]):
+                    left(relay_at(0, j), forward_sem.at[0, j])
+
+        for way in (0, 1):
+
+            @pl.when((x == column) & passes[way])
+            def _():
+                for j in range(way, COLUMN_PIECES[column], 2):
+                    left(relay_at(1, j), forward_sem.at[1, j])
+                if column == X - 1 and way == 0:
+                    left(len_relay, len_send.at[1])
+
     @pl.when(has_prev)
     def _():
-        for piece in range(N_PIECES):
-            arrived(prev_rows(core, piece), prev_sem.at[piece])
-            remote(
-                prev_rows(core, piece), prev_rows(core, piece), swap_send.at[piece], swap_recv.at[piece], sibling
-            ).start()
+        for index, column in enumerate(columns):
+            for j in range(COLUMN_PIECES[column]):
+                piece = PIECES[column, j]
+                arrived(prev_rows(core, piece), prev_sem.at[piece])
+            span = span_rows(core, column)
+            remote(span, span, swap_send.at[index], swap_recv.at[index], sibling).start()
         arrived(prev_len, len_recv.at[0])
         half = prev_ref.shape[1]
         project(prev_ref[core], 2, pl.multiple_of(core * half, half))
-        for piece in range(N_PIECES):
-            arrived(prev_rows(other, piece), swap_recv.at[piece])
+        for index, column in enumerate(columns):
+            arrived(span_rows(other, column), swap_recv.at[index])
         project(prev_ref[other], 2, pl.multiple_of(other * half, half))
         live = key_live(prev_len[1:2])
         row = lax.broadcasted_iota(jnp.int32, (16, HEAD_DIM), 0)
@@ -358,46 +386,19 @@
         for head, first in enumerate(attend(0, GROUP_LEN, 2, live)):
             at = pl.ds(head * HEAD_DIM, HEAD_DIM)
             out_ref[0, : GROUP_LEN - 16, at] = first[: GROUP_LEN - 16]
-            out_ref[0, edge, at] = jnp.where(row < 15, first[GROUP_LEN - 16 :], own_out[edge, at])
+            out_ref[0, edge, at] = jnp.where(row < 15, first[GROUP_LEN - 16 :], own_edge[:, at])
 
     @pl.when(jnp.logical_not(has_prev))
     def _():
-        row = lax.broadcasted_iota(jnp.int32, (16, own_out.shape[1]), 0)
+        row = lax.broadcasted_iota(jnp.int32, own_edge.shape, 0)
+        out_ref[0, : GROUP_LEN - 16] = jnp.zeros((GROUP_LEN - 16, own_edge.shape[1]), jnp.bfloat16)
         edge = pl.ds(GROUP_LEN - 16, 16)
-        out_ref[0, : GROUP_LEN - 16] = jnp.zeros((GROUP_LEN - 16, own_out.shape[1]), jnp.bfloat16)
-        out_ref[0, edge] = jnp.where(row < 15, jnp.zeros_like(row, jnp.bfloat16), own_out[edge])
-
-    out_ref[0, GROUP_LEN:] = own_out[GROUP_LEN:]
-
-    left(rows_ref.at[core], own_send)
-
-    @pl.when((x < X - 1) | (z < Z - 1) | (y < X - 1))
-    def _():
-        for piece in range(N_PIECES):
-            left(last_rows(piece), out_sem.at[piece])
-        left(len_ref, len_send.at[0])
-
-    for column in columns:
-        if column != X - 1:
-
-            @pl.when((x == column) & ((z < Z - 1) | (y < X - 1)))
-            def _():
-                for j in range(COLUMN_PIECES[column]):
-                    left(relay_at(0, j), forward_sem.at[0, j])
-
-        for way in (0, 1):
-
-            @pl.when((x == column) & passes[way])
-            def _():
-                for j in range(way, COLUMN_PIECES[column], 2):
-                    left(relay_at(1, j), forward_sem.at[1, j])
-                if column == X - 1 and way == 0:
-                    left(len_relay, len_send.at[1])
+        out_ref[0, edge] = jnp.where(row < 15, jnp.zeros_like(row, jnp.bfloat16), own_edge[...])
 
     @pl.when(has_prev)
     def _():
-        for piece in range(N_PIECES):
-            left(prev_rows(core, piece), swap_send.at[piece])
+        for index, column in enumerate(columns):
+            left(span_rows(core, column), swap_send.at[index])
 
 
 def shards(queries, encodings, neighbour_lengths, key_weight, value_weight):
@@ -421,7 +422,7 @@
             pltpu.VMEM((2, neighbours * half_rows, enc_width), bf16),
             pltpu.VMEM((3, 2 * neighbours * half_rows, col_count), bf16),
             pltpu.VMEM((3, 2 * neighbours * half_rows, col_count), bf16),
-            pltpu.VMEM((tok_count, col_count), bf16),
+            pltpu.VMEM((16, col_count), bf16),
             pltpu.VMEM((2, MOST * PIECE_ROWS, enc_width), bf16),
             pltpu.VMEM((group_count, neighbours), jnp.int32),
             dma((5,)),
@@ -429,8 +430,8 @@
             dma((2, MOST)),
             dma((2, MOST)),
             dma((N_PIECES,)),
-            dma((N_PIECES,)),
-            dma((N_PIECES,)),
+            dma((len(COLUMN_PIECES),)),
+            dma((len(COLUMN_PIECES),)),
             dma((2,)),
             dma((2,)),
             dma,

time: 42.7 us -> 41.5 us (0.972)
  the two profiles are of different devices: /device:TPU:57 before, /device:TPU:113 now
where the time goes in v4:
time: 41.5 us; the launch traced here: 41.4 us
  Pallas kernels  40.7 us (98%)
  local copies, waits for them, and re-layouts  0.71 us (2%)
    pallas_call x1, Pallas kernels, shards(): pl.pallas_call(kernel, out_shape=pltpu.VMEM(queries.shape, bf16), in_spec...  40.7 us

profile of v4, /device:TPU:113, one launch (start us, length us, event | category | flops | bytes accessed | tf_op | source)
XLA Modules:
  0.0 41.4 jit_solution(7989622006549634695)
XLA Ops:
  0.0 40.7 %attend_neighbours.1 = bf16[1,128,1024]{2,1,0:T(8,128)(2,1)S(1)} custom-call(bf16[1,128,1024]{2,1,0:T(8,128)(2,1)} %q_hbm.1, bf16[1,2,2,64,896]{4,3,2,1,0:T(8,128)(2,1)} %enc_hbm.1, s32[1,2,2]{2,1,0:T(2,128)} %len_hbm.1, bf16[896,1024]{1,0:T(8,128)(2,1)} %kw_hbm.1, bf16[896,1024]{1,0:T(8,128)(2,1)} %vw_hbm.1), custom_call_target="tpu_custom_call" | custom-call | tf_op jit(solution)/shard_map/attend_neighbours/pallas_call | solution.py:410
  40.7 0.7 %copy.7 = bf16[1,128,1024]{2,1,0:T(8,128)(2,1)} copy(bf16[1,128,1024]{2,1,0:T(8,128)(2,1)S(1)} %attend_neighbours.1) | data formatting | bytes 524288

commit v5 on v4

--- a/solution.py
+++ b/solution.py
@@ -12,7 +12,7 @@
 
 X, Z, HALF = 4, 32, 16
 COLUMN_PIECES = {3: 4, 0: 4, 2: 4, 1: 4}
-HOPS = (((0, 8, 8), (18,26,2)), ((0, 3, -4), (3, 8, 8), (18,26,2)))
+HOPS = (((0, 6, 8), (12, 13, -5), (19, 24, 2)), ((0, 3, -4), (3, 6, 8), (12, 13, -5), (19, 24, 2)))
 PIECE_ROWS = 8
 PIECES, SPANS = {}, {}
 for _column, _count in COLUMN_PIECES.items():

time: 41.5 us -> 41.1 us (level)
  the two profiles are of different devices: /device:TPU:113 before, /device:TPU:57 now
where the time goes in v5:
time: 41.1 us; the launch traced here: 41 us
  Pallas kernels  40.3 us (98%)
  local copies, waits for them, and re-layouts  0.71 us (2%)
    pallas_call x1, Pallas kernels, shards(): pl.pallas_call(kernel, out_shape=pltpu.VMEM(queries.shape, bf16), in_spec...  40.3 us

profile of v5, /device:TPU:57, one launch (start us, length us, event | category | flops | bytes accessed | tf_op | source)
XLA Modules:
  0.0 41.0 jit_solution(13872943368555197690)
XLA Ops:
  0.0 40.3 %attend_neighbours.1 = bf16[1,128,1024]{2,1,0:T(8,128)(2,1)S(1)} custom-call(bf16[1,128,1024]{2,1,0:T(8,128)(2,1)} %q_hbm.1, bf16[1,2,2,64,896]{4,3,2,1,0:T(8,128)(2,1)} %enc_hbm.1, s32[1,2,2]{2,1,0:T(2,128)} %len_hbm.1, bf16[896,1024]{1,0:T(8,128)(2,1)} %kw_hbm.1, bf16[896,1024]{1,0:T(8,128)(2,1)} %vw_hbm.1), custom_call_target="tpu_custom_call" | custom-call | tf_op jit(solution)/shard_map/attend_neighbours/pallas_call | solution.py:410
  40.3 0.7 %copy.7 = bf16[1,128,1024]{2,1,0:T(8,128)(2,1)} copy(bf16[1,128,1024]{2,1,0:T(8,128)(2,1)S(1)} %attend_neighbours.1) | data formatting | bytes 524288

commit v6 on v5

--- a/solution.py
+++ b/solution.py
@@ -401,13 +401,19 @@
             left(span_rows(core, column), swap_send.at[index])
 
 
+def write_out(from_ref, to_ref, sem):
+    copy = pltpu.make_async_copy(from_ref, to_ref, sem)
+    copy.start()
+    copy.wait()
+
+
 def shards(queries, encodings, neighbour_lengths, key_weight, value_weight):
     _, group_count, neighbours, half_rows, enc_width = encodings.shape
     tok_count, col_count = queries.shape[1:]
     bf16 = jnp.bfloat16
     anywhere = pl.BlockSpec(memory_space=pl.ANY)
     dma = pltpu.SemaphoreType.DMA
-    return pl.pallas_call(
+    attended = pl.pallas_call(
         kernel,
         out_shape=pltpu.VMEM(queries.shape, bf16),
         in_specs=[anywhere] * 5,
@@ -442,6 +448,15 @@
         ),
         name="attend_neighbours",
     )(queries, encodings, neighbour_lengths, key_weight, value_weight)
+    return pl.pallas_call(
+        write_out,
+        out_shape=jax.ShapeDtypeStruct(queries.shape, bf16),
+        in_specs=[anywhere],
+        out_specs=anywhere,
+        scratch_shapes=[dma],
+        compiler_params=pltpu.CompilerParams(vmem_limit_bytes=2**20),
+        name="write_out",
+    )(attended)
 
 
 def solution(mesh):

time: 41.1 us -> 41.1 us (level)
  local copies, waits for them, and re-layouts: 0.71 us -> 0 us
  Pallas kernels: 40.3 us -> 41 us
    pallas_call x0 -> x1, Pallas kernels: none -> 0.71 us  [shards(): pl.pallas_call(write_out, out_shape=jax.ShapeDtypeStruct(queries.shape, b...]
    unnamed x1 -> x0, local copies, waits for them, and re-layouts: 0.71 us -> none
where the time goes in v6:
time: 41.1 us; the launch traced here: 41 us
  Pallas kernels  41 us (100%)
    pallas_call x1, Pallas kernels, shards(): pl.pallas_call(kernel, out_shape=pltpu.VMEM(queries.shape, bf16), in_spec...  40.3 us

profile of v6, /device:TPU:57, one launch (start us, length us, event | category | flops | bytes accessed | tf_op | source)
XLA Modules:
  0.0 41.0 jit_solution(13498031889568192203)
XLA Ops:
  0.0 40.3 %attend_neighbours.1.from_ref = bf16[1,128,1024]{2,1,0:T(8,128)(2,1)S(1)} custom-call(bf16[1,128,1024]{2,1,0:T(8,128)(2,1)} %q_hbm.1, bf16[1,2,2,64,896]{4,3,2,1,0:T(8,128)(2,1)} %enc_hbm.1, s32[1,2,2]{2,1,0:T(2,128)} %len_hbm.1, bf16[896,1024]{1,0:T(8,128)(2,1)} %kw_hbm.1, bf16[896,1024]{1,0:T(8,128)(2,1)} %vw_hbm.1), custom_call_target="tpu_custom_call" | custom-call | tf_op jit(solution)/shard_map/attend_neighbours/pallas_call | solution.py:416
  40.3 0.7 %write_out.1 = bf16[1,128,1024]{2,1,0:T(8,128)(2,1)} custom-call(bf16[1,128,1024]{2,1,0:T(8,128)(2,1)S(1)} %attend_neighbours.1.from_ref), custom_call_target="tpu_custom_call" | custom-call | tf_op jit(solution)/shard_map/write_out/pallas_call | solution.py:451
